TPU v7x, 32 devices: a whole 2x2x4 slice. The times are simulated.
32 devices in a mesh: trc: 4 (over z), lat: 4 (over x, core), lon: 2 (over y).
Axes of the slice: x: 2, y: 2, z: 4, core: 2. Of those that a mesh axis runs over, the one named last changes fastest.
Arguments:
- species_concentrations: float32 [32, 8, 128, 256], P('trc', None, 'lat', 'lon'), may hold values from 0.2 to 4
- zonal_velocity_array: float32 [8, 128, 256], P('trc', 'lat', 'lon'), may hold values from -2.5 to 2.5
- meridional_velocity_array: float32 [8, 128, 256], P('trc', 'lat', 'lon'), may hold values from -2.5 to 2.5
- thermal_anomaly: float32 [8, 128, 256], P('trc', 'lat', 'lon'), may hold values from -6 to 6
- ocean_top_height_grid: float32 [128, 256], P('lat', 'lon'), may hold values from -6 to 6
- water_layer_tally: int32 [128, 256], P('lat', 'lon'), may hold values from 0 to 8
- species_interaction_table: float32 [32, 32], replicated, may hold values from -1 to 1
- species_production_pace: float32 [32], replicated, may hold values from 0.2 to 2
- photon_uptake: float32 [32], replicated, may hold values from 0.01 to 0.1
Outputs:
- updated_tracers: float32 [32, 8, 128, 256], P('trc', None, 'lat', 'lon')
- east_out: float32 [8, 128, 256], P('trc', 'lat', 'lon')
- north_out: float32 [8, 128, 256], P('trc', 'lat', 'lon')
- temperature_out: float32 [8, 128, 256], P('trc', 'lat', 'lon')
- height_out: float32 [128, 256], P('lat', 'lon')
Inputs may be any that keep to these rules, and one draw needn't show every extreme that they name: `water_layer_tally`: the number of wet levels of a column, counted from the surface; cells below it, and whole columns with 0, are land.
All inputs are finite; a program needn't handle non-finite values.
Results may differ from a plain program's by a relative error of at most 0.0003.
Values sent between devices are 32-bit elements; how exact they have to be, the bound alone decides.
No kernel may reach another device: no remote copies, remote signals or barrier semaphores. Data moves between devices by JAX's collectives and lax.ppermute only.
A program may use at most 64 MiB of HBM per device.

v0:
```python
import math
import jax
import jax.numpy as jnp
from jax import lax
from jax.sharding import PartitionSpec as P

HIGHEST = lax.Precision.HIGHEST
TIME_STEP = 0.1
GRAVITY = 1.0
VISCOSITY = 0.2
BOTTOM_DRAG = 0.05
DEPTH_SCALE = 0.5
CORIOLIS_SCALE = 0.5
COLUMN_DEPTH = 2.0
WATER_ABSORB = 0.2
HALF_LIGHT = 0.5
REACT_STEP = 0.1
WARMING_WEIGHT = 1.0


def padded(block, sides, width, periodic):
    for axis, dim in sides:
        count = lax.axis_size(axis)
        forward = [(i, i + 1) for i in range(count - 1)]
        if periodic:
            forward.append((count - 1, 0))
        backward = [(target, source) for source, target in forward]
        low = lax.ppermute(
            lax.slice_in_dim(block, block.shape[dim] - width, None, axis=dim), axis, forward
        )
        high = lax.ppermute(lax.slice_in_dim(block, 0, width, axis=dim), axis, backward)
        block = jnp.concatenate([low, block, high], axis=dim)
    return block


def limited_slope(ahead, behind):
    smaller = jnp.minimum(jnp.abs(ahead), jnp.abs(behind))
    return jnp.where(
        ahead * behind > 0, jnp.where(ahead > 0, smaller, -smaller), jnp.zeros_like(smaller)
    )


def face_flux(before, center, after, beyond, vel_here, vel_next, wet_here, wet_next):
    courant = 0.5 * (vel_here + vel_next) * wet_here * wet_next
    upwind_pos = center + 0.5 * (1.0 - courant) * limited_slope(after - center, center - before)
    upwind_neg = after - 0.5 * (1.0 + courant) * limited_slope(beyond - after, after - center)
    return courant * jnp.where(courant >= 0, upwind_pos, upwind_neg)


def transport(field, flow_east, flow_north, wet):
    free_top_height, width = (field.shape[-2], field.shape[-1])
    rows = slice(2, free_top_height - 2)
    cols = slice(2, width - 2)
    flux_x = face_flux(
        field[..., rows, 0 : width - 3],
        field[..., rows, 1 : width - 2],
        field[..., rows, 2 : width - 1],
        field[..., rows, 3:width],
        flow_east[..., rows, 1 : width - 2],
        flow_east[..., rows, 2 : width - 1],
        wet[..., rows, 1 : width - 2],
        wet[..., rows, 2 : width - 1],
    )
    flux_y = face_flux(
        field[..., 0 : free_top_height - 3, cols],
        field[..., 1 : free_top_height - 2, cols],
        field[..., 2 : free_top_height - 1, cols],
        field[..., 3:free_top_height, cols],
        flow_north[..., 1 : free_top_height - 2, cols],
        flow_north[..., 2 : free_top_height - 1, cols],
        wet[..., 1 : free_top_height - 2, cols],
        wet[..., 2 : free_top_height - 1, cols],
    )
    return (
        field[..., rows, cols]
        - (flux_x[..., 1:] - flux_x[..., :-1])
        - (flux_y[..., 1:, :] - flux_y[..., :-1, :])
    )


def ocean_core(stacked, north, south, east, west, wet, coriolis):
    count = (stacked.shape[0] - 1) // 2
    zonal_flow_value = stacked[:count]
    meridional_flow_value = stacked[count : 2 * count]
    free_top_height = stacked[2 * count]
    lap_east = north[:count] + south[:count] + east[:count] + west[:count] - 4.0 * zonal_flow_value
    lap_north = (
        north[count : 2 * count]
        + south[count : 2 * count]
        + east[count : 2 * count]
        + west[count : 2 * count]
        - 4.0 * meridional_flow_value
    )
    grad_x = 0.5 * (east[2 * count] - west[2 * count])
    grad_y = 0.5 * (north[2 * count] - south[2 * count])
    div_levels = 0.5 * (east[:count] - west[:count]) + 0.5 * (
        north[count : 2 * count] - south[count : 2 * count]
    )
    new_east = wet * (
        zonal_flow_value
        + TIME_STEP
        * (
            coriolis * meridional_flow_value
            - GRAVITY * grad_x
            + VISCOSITY * lap_east
            - BOTTOM_DRAG * zonal_flow_value
        )
    )
    new_north = wet * (
        meridional_flow_value
        + TIME_STEP
        * (
            -coriolis * zonal_flow_value
            - GRAVITY * grad_y
            + VISCOSITY * lap_north
            - BOTTOM_DRAG * meridional_flow_value
        )
    )
    return (new_east, new_north, free_top_height, jnp.sum(div_levels, 0))


def ocean_step(zonal_flow_value, meridional_flow_value, free_top_height, wet, coriolis):
    stacked = jnp.concatenate([zonal_flow_value, meridional_flow_value, free_top_height[None]], 0)
    by_lat = padded(stacked, (("lat", 1),), 1, False)
    by_lon = padded(stacked, (("lon", 2),), 1, True)
    new_east, new_north, free_top_height, partial_div = ocean_core(
        stacked,
        by_lat[:, 2:, :],
        by_lat[:, :-2, :],
        by_lon[:, :, 2:],
        by_lon[:, :, :-2],
        wet,
        coriolis,
    )
    divergence = lax.psum(partial_div, "trc")
    return (new_east, new_north, free_top_height - TIME_STEP * DEPTH_SCALE * divergence)


def widen_flow(flow, width):
    rows_ext = padded(flow, (("lat", 2),), width, False)
    return padded(rows_ext, (("lon", 3),), width, True)


def widen_tracers(field, width):
    rows_ext = padded(field, (("lat", 2),), width, False)
    return padded(rows_ext, (("lon", 3),), width, True)


def light_profile(absorbed, wet, surface):
    levels = absorbed.shape[0]
    layer = COLUMN_DEPTH / levels * (WATER_ABSORB + absorbed) * wet
    above = jnp.cumsum(layer, 0) - layer
    top_light = surface[None, :, None] * jnp.exp(-above)
    return (top_light * (1.0 - jnp.exp(-layer)), top_light / (top_light + HALF_LIGHT))


def body(
    species_concentrations,
    zonal_velocity_array,
    meridional_velocity_array,
    thermal_anomaly,
    ocean_top_height_grid,
    water_layer_tally,
    species_interaction_table,
    species_production_pace,
    photon_uptake,
):
    tracer_count, levels, lat_rows, lon_cols = species_concentrations.shape
    own_levels = zonal_velocity_array.shape[0]
    trc_place = lax.axis_index("trc")
    lat_total = lat_rows * lax.axis_size("lat")
    lat_global = (lax.axis_index("lat") * lat_rows + jnp.arange(lat_rows)).astype(jnp.float32)
    angle = math.pi * ((lat_global + 0.5) / lat_total - 0.5)
    coriolis = CORIOLIS_SCALE * jnp.sin(angle)[:, None]
    surface = 1.0 + jnp.cos(angle)
    depth_index = jnp.arange(levels)
    wet_all = (depth_index[:, None, None] < water_layer_tally[None]).astype(jnp.float32)
    wet_own = lax.dynamic_slice_in_dim(wet_all, trc_place * own_levels, own_levels, 0)
    east_start = wet_own * zonal_velocity_array
    north_start = wet_own * meridional_velocity_array
    zonal_flow_value, meridional_flow_value, free_top_height = (
        east_start,
        north_start,
        ocean_top_height_grid,
    )
    for substep in range(2):
        zonal_flow_value, meridional_flow_value, free_top_height = ocean_step(
            zonal_flow_value, meridional_flow_value, free_top_height, wet_own, coriolis
        )
    velocity = lax.all_gather(jnp.stack([east_start, north_start]), "trc", axis=1, tiled=True)
    flow = jnp.concatenate([velocity, wet_all[None]], 0)
    flow_ext = widen_flow(flow, 4)
    first = transport(
        widen_tracers(species_concentrations, 4), flow_ext[0], flow_ext[1], flow_ext[2]
    )
    inner = flow_ext[:, :, 2:-2, 2:-2]
    moved = transport(first, inner[0], inner[1], inner[2])
    share = lat_rows // lax.axis_size("trc")
    columns = lax.all_to_all(moved, "trc", split_axis=2, concat_axis=0, tiled=True)
    wet_cols = lax.dynamic_slice_in_dim(wet_all, trc_place * share, share, 1)
    surface_cols = lax.dynamic_slice_in_dim(surface, trc_place * share, share, 0)
    absorbed = jnp.einsum("n,nkyx->kyx", photon_uptake, jnp.abs(columns), precision=HIGHEST)
    solar_warming, light_factor = light_profile(absorbed, wet_cols, surface_cols)
    mixed = jnp.einsum("mn,nkyx->mkyx", species_interaction_table, columns, precision=HIGHEST)
    species_postchemistry = columns + wet_cols * REACT_STEP * (
        mixed + species_production_pace[:, None, None, None] * light_factor * columns
    )
    updated_tracers = lax.all_to_all(
        species_postchemistry, "trc", split_axis=0, concat_axis=2, tiled=True
    )
    pointwise_warming_pace = lax.all_to_all(
        solar_warming, "trc", split_axis=0, concat_axis=1, tiled=True
    )
    return (
        updated_tracers,
        zonal_flow_value,
        meridional_flow_value,
        thermal_anomaly + WARMING_WEIGHT * pointwise_warming_pace,
        free_top_height,
    )


def solution(mesh):
    return jax.shard_map(
        body,
        mesh=mesh,
        in_specs=(
            P("trc", None, "lat", "lon"),
            P("trc", "lat", "lon"),
            P("trc", "lat", "lon"),
            P("trc", "lat", "lon"),
            P("lat", "lon"),
            P("lat", "lon"),
            P(),
            P(),
            P(),
        ),
        out_specs=(
            P("trc", None, "lat", "lon"),
            P("trc", "lat", "lon"),
            P("trc", "lat", "lon"),
            P("trc", "lat", "lon"),
            P("lat", "lon"),
        ),
        check_vma=False,
    )
```

profile of v0, /device:TPU:0, one launch (start us, length us, event | category | flops | bytes accessed | tf_op | source)
XLA Modules:
  0.0 207.8 jit_solution(16878511505992361957)
XLA Ops:
  3.0 15.7 %all_gather.3 = f32[2,8,32,128]{3,2,0,1:T(8,128)S(1)} all-gather(f32[2,2,32,128]{3,2,0,1:T(8,128)S(1)} %pad_maximum_fusion.8), channel_id=1, replica_groups=mesh['trc'=4,'lat'=4,'lon'=2] {'trc'}, dimensions={1}, use_global_device_ids=true | all-gather | bytes 327680 | tf_op jit(solution)/shard_map/all_gather | solution.py:190
  18.9 1.3 collective-permute-start.5
  20.2 3.0 %collective-permute-start.4 = (f32[3,8,4,128]{3,1,2,0:T(8,128)S(1)}, f32[3,8,4,128]{3,1,2,0:T(8,128)S(1)}, u32[]{:S(2)}, u32[]{:S(2)}) collective-permute-start(f32[3,8,4,128]{3,1,2,0:T(8,128)S(1)} %get-tuple-element.30), channel_id=1, source_target_pairs={{0,2},{2,4},{4,6},{1,3},{3,5},{5,7},{8,10},{10,12},{12,14},{9,11},... | collective-permute-start | bytes 147464 | tf_op jit(solution)/shard_map/ppermute | solution.py:28
  25.0 1.5 collective-permute-start.7
  27.8 1.3 collective-permute-start.1
  29.7 4.0 %collective-permute-start = (f32[8,8,4,128]{3,1,2,0:T(8,128)}, f32[8,8,4,128]{3,1,2,0:T(8,128)}, u32[]{:S(2)}, u32[]{:S(2)}) collective-permute-start(f32[8,8,4,128]{3,1,2,0:T(8,128)} %copy.159), channel_id=1, source_target_pairs={{0,2},{2,4},{4,6},{1,3},{3,5},{5,7},{8,10},{10,12},{12,14},{9,11},... | collective-permute-start | bytes 393224 | tf_op jit(solution)/shard_map/ppermute | solution.py:28
  33.7 2.7 %copy.131 = f32[8,8,32,128]{2,1,3,0:T(8,128)} copy(f32[8,8,32,128]{3,2,1,0:T(8,128)S(1)} %copy-done.8) | data formatting | bytes 2097152 | tf_op args[0]
  36.4 2.5 %collective-permute-done.7 = f32[3,8,40,4]{3,1,2,0:T(8,128)S(1)} collective-permute-done((f32[3,8,40,4]{3,1,2,0:T(8,128)}, f32[3,8,40,4]{3,1,2,0:T(8,128)S(1)}, u32[]{:S(2)}, u32[]{:S(2)}) %collective-permute-start.7) | collective-permute-done | bytes 15392 | tf_op jit(solution)/shard_map/ppermute | solution.py:31
  38.9 10.5 %collective-permute-done.6 = f32[3,8,40,4]{3,1,2,0:T(8,128)S(1)} collective-permute-done((f32[3,8,40,4]{3,1,2,0:T(8,128)S(1)}, f32[3,8,40,4]{3,1,2,0:T(8,128)S(1)}, u32[]{:S(2)}, u32[]{:S(2)}) %collective-permute-start.6) | collective-permute-done | bytes 15392 | tf_op jit(solution)/shard_map/ppermute | solution.py:28
  55.2 3.6 %copy.132 = f32[8,8,4,128]{2,1,3,0:T(8,128)} copy(f32[8,8,4,128]{3,1,2,0:T(8,128)} %collective-permute-done.1) | data formatting | bytes 262144 | tf_op jit(solution)/shard_map/ppermute | solution.py:31
  58.8 3.5 %copy.130 = f32[8,8,4,128]{2,1,3,0:T(8,128)} copy(f32[8,8,4,128]{3,1,2,0:T(8,128)} %collective-permute-done) | data formatting | bytes 262144 | tf_op jit(solution)/shard_map/ppermute | solution.py:28
  62.3 2.1 %pad_maximum_fusion.5 = (f32[8,8,40,4]{2,1,3,0:T(8,128)}, f32[8,8,40,4]{2,1,3,0:T(8,128)}) fusion(f32[8,8,4,128]{2,1,3,0:T(8,128)} %copy.132, f32[8,8,32,128]{2,1,3,0:T(8,128)} %copy.131, f32[8,8,4,128]{2,1,3,0:T(8,128)} %copy.130), kind=kLoop, calls=%fused_computation.120 | loop fusion | flops 40960 | bytes 1392640 | tf_op jit(solution)/shard_map/slice | solution.py:29
  64.4 1.5 collective-permute-start.3
  69.0 1.2 copy.143
  70.6 1.2 copy.141
  72.3 1.4 copy.138
  73.6 1.4 copy.137
  75.0 1.3 copy.136
  76.3 1.9 copy.150
  80.4 2.1 %copy.146 = f32[8,32,129]{1,0,2:T(8,128)} copy(f32[8,32,129]{2,0,1:T(8,128)} %get-tuple-element.37) | data formatting | bytes 264192 | tf_op jit(solution)/shard_map/mul | solution.py:46
  82.5 2.1 %copy.145 = f32[8,32,129]{1,0,2:T(8,128)} copy(f32[8,32,129]{2,0,1:T(8,128)} %get-tuple-element.36) | data formatting | bytes 264192 | tf_op jit(solution)/shard_map/mul | solution.py:45
  84.6 1.2 copy.144
  85.9 6.0 %pad_maximum_fusion = f32[8,8,40,136]{2,1,3,0:T(8,128)S(1)} fusion(f32[8,8,40,4]{2,1,3,0:T(8,128)} %collective-permute-done.3, f32[8,8,4,128]{2,1,3,0:T(8,128)} %copy.132, f32[8,8,32,128]{2,1,3,0:T(8,128)} %copy.131, f32[8,8,4,128]{2,1,3,0:T(8,128)} %copy.130, f32[8,8,40,4]{2,1,3,0:T(8,128)} %collective-permute-done.2), kind=kLoop, calls=%fused_computation.8 | loop fusion | flops 1392640 | bytes 2785280 | tf_op jit(solution)/shard_map/concatenate | solution.py:32
  91.8 4.3 %fusion.12 = f32[8,8,37,132]{2,1,3,0:T(8,128)S(1)} fusion(f32[8,8,40,136]{2,1,3,0:T(8,128)S(1)} %pad_maximum_fusion, f32[8,37,132]{1,0,2:T(8,128)S(1)} %copy.142, f32[8,37,132]{1,0,2:T(8,128)S(1)} %copy-done.1, f32[8,37,132]{1,0,2:T(8,128)S(1)} %copy.139, pred[8,37,132]{1,0,2:T(8,128)(4,1)S(1)} %copy.140), kind=kLoop, calls=%fused_computation.26 | loop fusion | flops 8126976 | bytes 6759456 | tf_op jit(solution)/shard_map/mul | solution.py:47
  96.1 5.1 %fusion.4 = f32[8,8,36,133]{2,1,3,0:T(8,128)S(1)} fusion(f32[8,8,40,136]{2,1,3,0:T(8,128)S(1)} %pad_maximum_fusion, f32[8,36,133]{1,0,2:T(8,128)S(1)} %copy.138, f32[8,36,133]{1,0,2:T(8,128)S(1)} %copy.137, f32[8,36,133]{1,0,2:T(8,128)S(1)} %copy.135, pred[8,36,133]{1,0,2:T(8,128)(4,1)S(1)} %copy.136), kind=kLoop, calls=%fused_computation.13 | loop fusion | flops 7967232 | bytes 6626592 | tf_op jit(solution)/shard_map/mul | solution.py:47
  101.3 2.6 %fusion.16 = f32[8,8,36,132]{2,1,3,0:T(8,128)S(1)} fusion(f32[8,8,37,132]{2,1,3,0:T(8,128)S(1)} %fusion.12, f32[8,8,36,133]{2,1,3,0:T(8,128)S(1)} %fusion.4, f32[8,8,40,136]{2,1,3,0:T(8,128)S(1)} %pad_maximum_fusion), kind=kLoop, calls=%fused_computation.31 | loop fusion | flops 1216512 | bytes 7299072 | tf_op jit(solution)/shard_map/sub | solution.py:75
  103.9 4.2 %fusion.30 = f32[8,8,33,128]{2,1,3,0:T(8,128)S(1)} fusion(f32[8,8,36,132]{2,1,3,0:T(8,128)S(1)} %fusion.16, f32[8,33,128]{1,0,2:T(8,128)S(1)} %copy-done.6, f32[8,33,128]{1,0,2:T(8,128)S(1)} %copy-done.7, f32[8,33,128]{1,0,2:T(8,128)S(1)} %copy-done.5, pred[8,33,128]{1,0,2:T(8,128)(4,1)S(1)} %copy.148), kind=kLoop, calls=%fused_computation.56 | loop fusion | flops 7028736 | bytes 5846016 | tf_op jit(solution)/shard_map/mul | solution.py:47
  108.1 4.7 %fusion.22 = f32[8,8,32,129]{2,1,3,0:T(8,128)S(1)} fusion(f32[8,8,36,132]{2,1,3,0:T(8,128)S(1)} %fusion.16, f32[8,32,129]{1,0,2:T(8,128)S(1)} %copy-done.3, f32[8,32,129]{1,0,2:T(8,128)S(1)} %copy-done.4, f32[8,32,129]{1,0,2:T(8,128)S(1)} %copy-done.2, pred[8,32,129]{1,0,2:T(8,128)(4,1)S(1)} %copy.144), kind=kLoop, calls=%fused_computation.43 | loop fusion | flops 6868992 | bytes 5713152 | tf_op jit(solution)/shard_map/mul | solution.py:47
  112.9 3.8 %fusion.34 = f32[8,8,32,128]{2,1,3,0:T(8,128)} fusion(f32[8,8,33,128]{2,1,3,0:T(8,128)S(1)} %fusion.30, f32[8,8,32,129]{2,1,3,0:T(8,128)S(1)} %fusion.22, f32[8,8,36,132]{2,1,3,0:T(8,128)S(1)} %fusion.16), kind=kLoop, calls=%fused_computation.61 | loop fusion | flops 1048576 | bytes 6291456 | tf_op jit(solution)/shard_map/sub | solution.py:75
  116.6 3.9 %copy.151 = f32[8,8,32,128]{3,1,0,2:T(8,128)} copy(f32[8,8,32,128]{2,1,3,0:T(8,128)} %fusion.34) | data formatting | bytes 2097152 | tf_op jit(solution)/shard_map/sub | solution.py:75
  120.6 5.2 %all-to-all-start = ((f32[8,8,32,128]{3,1,0,2:T(8,128)}), f32[8,8,32,128]{3,1,0,2:T(8,128)S(1)}, u32[]{:S(2)}, u32[]{:S(2)}) async-start(f32[8,8,32,128]{3,1,0,2:T(8,128)} %copy.151), calls=%async_computation | async-start | bytes 2097152 | tf_op jit(solution)/shard_map/all_to_all | solution.py:199
  125.8 1.3 collective-permute-start.11
  127.1 1.3 collective-permute-start.10
  128.5 1.6 collective-permute-start.9
  130.8 2.2 %collective-permute-done.9 = f32[5,32,1]{2,1,0:T(8,128)S(1)} collective-permute-done((f32[5,32,1]{2,1,0:T(8,128)S(1)}, f32[5,32,1]{2,1,0:T(8,128)S(1)}, u32[]{:S(2)}, u32[]{:S(2)}) %collective-permute-start.9) | collective-permute-done | bytes 672 | tf_op jit(solution)/shard_map/ppermute | solution.py:28
  133.0 2.2 %collective-permute-done.8 = f32[5,32,1]{2,1,0:T(8,128)S(1)} collective-permute-done((f32[5,32,1]{2,1,0:T(8,128)S(1)}, f32[5,32,1]{2,1,0:T(8,128)S(1)}, u32[]{:S(2)}, u32[]{:S(2)}) %collective-permute-start.8) | collective-permute-done | bytes 672 | tf_op jit(solution)/shard_map/ppermute | solution.py:31
  135.4 24.5 %psum.14 = f32[32,128]{1,0:T(8,128)S(1)} all-reduce(f32[32,128]{1,0:T(8,128)S(1)} %multiply_reduce_fusion.1), channel_id=1, replica_groups=mesh['trc'=4,'lat'=4,'lon'=2] {'trc'}, use_global_device_ids=true, to_apply=%region_2.0 | all-reduce | flops 4096 | bytes 32768 | tf_op jit(solution)/shard_map/psum | solution.py:135
  161.7 3.4 %all-to-all-start.2 = ((f32[8,8,128]{2,1,0:T(8,128)}), f32[8,8,128]{2,1,0:T(8,128)S(1)}, u32[]{:S(2)}, u32[]{:S(2)}) async-start(f32[8,8,128]{2,1,0:T(8,128)} %get-tuple-element.40), calls=%async_computation.2 | async-start | bytes 65536 | tf_op jit(solution)/shard_map/all_to_all | solution.py:211
  165.1 1.3 fusion.38
  166.4 1.6 copy.153
  168.0 2.7 %all-to-all-done.2 = f32[8,8,128]{2,1,0:T(8,128)S(1)} async-done(((f32[8,8,128]{2,1,0:T(8,128)}), f32[8,8,128]{2,1,0:T(8,128)S(1)}, u32[]{:S(2)}, u32[]{:S(2)}) %all-to-all-start.2) | async-done | bytes 32800 | tf_op jit(solution)/shard_map/all_to_all | solution.py:211
  170.7 3.5 %all-to-all-start.1 = ((f32[32,8,8,128]{3,2,1,0:T(8,128)}), f32[32,8,8,128]{3,2,1,0:T(8,128)S(1)}, u32[]{:S(2)}, u32[]{:S(2)}) async-start(f32[32,8,8,128]{3,2,1,0:T(8,128)} %copy.153), calls=%async_computation.1 | async-start | bytes 2097152 | tf_op jit(solution)/shard_map/all_to_all | solution.py:208
  174.3 1.3 collective-permute-start.15
  175.6 1.3 collective-permute-start.14
  177.0 1.6 collective-permute-start.13
  179.1 3.1 %collective-permute-done.13 = f32[5,32,1]{2,1,0:T(8,128)S(1)} collective-permute-done((f32[5,32,1]{2,1,0:T(8,128)S(1)}, f32[5,32,1]{2,1,0:T(8,128)S(1)}, u32[]{:S(2)}, u32[]{:S(2)}) %collective-permute-start.13) | collective-permute-done | bytes 672 | tf_op jit(solution)/shard_map/ppermute | solution.py:28
  182.2 1.8 collective-permute-done.12
  184.1 19.9 %psum.15 = f32[32,128]{1,0:T(8,128)S(1)} all-reduce(f32[32,128]{1,0:T(8,128)S(1)} %multiply_reduce_fusion), channel_id=1, replica_groups=mesh['trc'=4,'lat'=4,'lon'=2] {'trc'}, use_global_device_ids=true, to_apply=%region_4.5 | all-reduce | flops 4096 | bytes 32768 | tf_op jit(solution)/shard_map/psum | solution.py:135
  (96 shorter events, 25.3 us)
Async XLA Ops:
  0.6 164.5 %copy-start = (f32[32,32]{1,0:T(8,128)S(1)}, f32[32,32]{1,0:T(8,128)}, u32[]{:S(2)}) copy-start(f32[32,32]{1,0:T(8,128)} %param.15) | copy-start | bytes 12292
  0.6 26.4 %copy-start.8 = (f32[8,8,32,128]{3,2,1,0:T(8,128)S(1)}, f32[8,8,32,128]{3,2,1,0:T(8,128)}, u32[]{:S(2)}) copy-start(f32[8,8,32,128]{3,2,1,0:T(8,128)} %param.9) | copy-start | bytes 3145732
  18.9 4.3 %collective-permute-start.5 = (f32[3,8,4,128]{3,1,2,0:T(8,128)S(1)}, f32[3,8,4,128]{3,1,2,0:T(8,128)S(1)}, u32[]{:S(2)}, u32[]{:S(2)}) collective-permute-start(f32[3,8,4,128]{3,1,2,0:T(8,128)S(1)} %get-tuple-element.31), channel_id=1, source_target_pairs={{2,0},{4,2},{6,4},{3,1},{5,3},{7,5},{10,8},{12,10},{14,12},{11,9},... | collective-permute-start | bytes 147464 | tf_op jit(solution)/shard_map/ppermute | solution.py:31
  20.2 3.9 %collective-permute-start.4 = (f32[3,8,4,128]{3,1,2,0:T(8,128)S(1)}, f32[3,8,4,128]{3,1,2,0:T(8,128)S(1)}, u32[]{:S(2)}, u32[]{:S(2)}) collective-permute-start(f32[3,8,4,128]{3,1,2,0:T(8,128)S(1)} %get-tuple-element.30), channel_id=1, source_target_pairs={{0,2},{2,4},{4,6},{1,3},{3,5},{5,7},{8,10},{10,12},{12,14},{9,11},... | collective-permute-start | bytes 147464 | tf_op jit(solution)/shard_map/ppermute | solution.py:28
  25.0 13.9 %collective-permute-start.7 = (f32[3,8,40,4]{3,1,2,0:T(8,128)}, f32[3,8,40,4]{3,1,2,0:T(8,128)S(1)}, u32[]{:S(2)}, u32[]{:S(2)}) collective-permute-start(f32[3,8,40,4]{3,1,2,0:T(8,128)} %get-tuple-element.29), channel_id=1, source_target_pairs={{1,0},{0,1},{3,2},{2,3},{5,4},{4,5},{7,6},{6,7},{9,8},{8,9},{11,10... | collective-permute-start | bytes 46088 | tf_op jit(solution)/shard_map/ppermute | solution.py:31
  26.5 22.9 %collective-permute-start.6 = (f32[3,8,40,4]{3,1,2,0:T(8,128)S(1)}, f32[3,8,40,4]{3,1,2,0:T(8,128)S(1)}, u32[]{:S(2)}, u32[]{:S(2)}) collective-permute-start(f32[3,8,40,4]{3,1,2,0:T(8,128)S(1)} %get-tuple-element.28), channel_id=1, source_target_pairs={{0,1},{1,0},{2,3},{3,2},{4,5},{5,4},{6,7},{7,6},{8,9},{9,8},{10,11... | collective-permute-start | bytes 46088 | tf_op jit(solution)/shard_map/ppermute | solution.py:28
  27.8 27.4 %collective-permute-start.1 = (f32[8,8,4,128]{3,1,2,0:T(8,128)}, f32[8,8,4,128]{3,1,2,0:T(8,128)}, u32[]{:S(2)}, u32[]{:S(2)}) collective-permute-start(f32[8,8,4,128]{3,1,2,0:T(8,128)} %copy.160), channel_id=1, source_target_pairs={{2,0},{4,2},{6,4},{3,1},{5,3},{7,5},{10,8},{12,10},{14,12},{11,9},... | collective-permute-start | bytes 393224 | tf_op jit(solution)/shard_map/ppermute | solution.py:31
  29.7 29.1 %collective-permute-start = (f32[8,8,4,128]{3,1,2,0:T(8,128)}, f32[8,8,4,128]{3,1,2,0:T(8,128)}, u32[]{:S(2)}, u32[]{:S(2)}) collective-permute-start(f32[8,8,4,128]{3,1,2,0:T(8,128)} %copy.159), channel_id=1, source_target_pairs={{0,2},{2,4},{4,6},{1,3},{3,5},{5,7},{8,10},{10,12},{12,14},{9,11},... | collective-permute-start | bytes 393224 | tf_op jit(solution)/shard_map/ppermute | solution.py:28
  64.4 21.4 %collective-permute-start.3 = (f32[8,8,40,4]{2,1,3,0:T(8,128)}, f32[8,8,40,4]{2,1,3,0:T(8,128)}, u32[]{:S(2)}, u32[]{:S(2)}) collective-permute-start(f32[8,8,40,4]{2,1,3,0:T(8,128)} %get-tuple-element.19), channel_id=1, source_target_pairs={{1,0},{0,1},{3,2},{2,3},{5,4},{4,5},{7,6},{6,7},{9,8},{8,9},{11,10... | collective-permute-start | bytes 122888 | tf_op jit(solution)/shard_map/ppermute | solution.py:31
  65.9 19.9 %collective-permute-start.2 = (f32[8,8,40,4]{2,1,3,0:T(8,128)}, f32[8,8,40,4]{2,1,3,0:T(8,128)}, u32[]{:S(2)}, u32[]{:S(2)}) collective-permute-start(f32[8,8,40,4]{2,1,3,0:T(8,128)} %get-tuple-element.18), channel_id=1, source_target_pairs={{0,1},{1,0},{2,3},{3,2},{4,5},{5,4},{6,7},{7,6},{8,9},{9,8},{10,11... | collective-permute-start | bytes 122888 | tf_op jit(solution)/shard_map/ppermute | solution.py:28
  70.2 8.0 %copy-start.10 = (f32[8,33,128]{2,0,1:T(8,128)S(1)}, f32[8,33,128]{2,0,1:T(8,128)}, u32[]{:S(2)}) copy-start(f32[8,33,128]{2,0,1:T(8,128)} %get-tuple-element.38) | copy-start | bytes 405508
  85.8 6.0 %copy-start.1 = (f32[8,37,132]{1,0,2:T(8,128)S(1)}, f32[8,37,132]{1,0,2:T(8,128)}, u32[]{:S(2)}) copy-start(f32[8,37,132]{1,0,2:T(8,128)} %copy.141) | copy-start | bytes 468868
  101.2 2.6 %copy-start.5 = (f32[8,33,128]{1,0,2:T(8,128)S(1)}, f32[8,33,128]{1,0,2:T(8,128)}, u32[]{:S(2)}) copy-start(f32[8,33,128]{1,0,2:T(8,128)} %copy.147) | copy-start | bytes 405508
  101.3 2.6 %copy-start.6 = (f32[8,33,128]{1,0,2:T(8,128)S(1)}, f32[8,33,128]{1,0,2:T(8,128)}, u32[]{:S(2)}) copy-start(f32[8,33,128]{1,0,2:T(8,128)} %copy.150) | copy-start | bytes 405508
  101.3 2.6 %copy-start.7 = (f32[8,33,128]{1,0,2:T(8,128)S(1)}, f32[8,33,128]{1,0,2:T(8,128)}, u32[]{:S(2)}) copy-start(f32[8,33,128]{1,0,2:T(8,128)} %copy.149) | copy-start | bytes 405508
  103.9 4.3 %copy-start.2 = (f32[8,32,129]{1,0,2:T(8,128)S(1)}, f32[8,32,129]{1,0,2:T(8,128)}, u32[]{:S(2)}) copy-start(f32[8,32,129]{1,0,2:T(8,128)} %copy.143) | copy-start | bytes 396292
  103.9 4.3 %copy-start.3 = (f32[8,32,129]{1,0,2:T(8,128)S(1)}, f32[8,32,129]{1,0,2:T(8,128)}, u32[]{:S(2)}) copy-start(f32[8,32,129]{1,0,2:T(8,128)} %copy.146) | copy-start | bytes 396292
  103.9 4.3 %copy-start.4 = (f32[8,32,129]{1,0,2:T(8,128)S(1)}, f32[8,32,129]{1,0,2:T(8,128)}, u32[]{:S(2)}) copy-start(f32[8,32,129]{1,0,2:T(8,128)} %copy.145) | copy-start | bytes 396292
  116.6 9.1 %copy-start.9 = (f32[32,128]{1,0:T(8,128)S(1)}, f32[32,128]{1,0:T(8,128)}, u32[]{:S(2)}) copy-start(f32[32,128]{1,0:T(8,128)} %param.13) | copy-start | bytes 49156
  116.6 43.5 %copy-start.12 = (f32[32]{0:T(128)S(1)}, f32[32]{0:T(128)}, u32[]{:S(2)}) copy-start(f32[32]{0:T(128)} %param.17) | copy-start | bytes 388
  116.6 48.5 %copy-start.13 = (f32[32]{0:T(128)S(1)}, f32[32]{0:T(128)}, u32[]{:S(2)}) copy-start(f32[32]{0:T(128)} %param.16) | copy-start | bytes 388
  120.6 39.6 %all-to-all-start = ((f32[8,8,32,128]{3,1,0,2:T(8,128)}), f32[8,8,32,128]{3,1,0,2:T(8,128)S(1)}, u32[]{:S(2)}, u32[]{:S(2)}) async-start(f32[8,8,32,128]{3,1,0,2:T(8,128)} %copy.151), calls=%async_computation | async-start | bytes 2097152 | tf_op jit(solution)/shard_map/all_to_all | solution.py:199
  125.8 9.5 %collective-permute-start.11 = (f32[5,1,128]{2,1,0:T(1,128)S(1)}, f32[5,1,128]{2,1,0:T(1,128)S(1)}, u32[]{:S(2)}, u32[]{:S(2)}) collective-permute-start(f32[5,1,128]{2,1,0:T(1,128)S(1)} %get-tuple-element.55), channel_id=1, source_target_pairs={{0,2},{2,4},{4,6},{1,3},{3,5},{5,7},{8,10},{10,12},{12,14},{9,11},... | collective-permute-start | bytes 7688 | tf_op jit(solution)/shard_map/ppermute | solution.py:28
  127.1 8.2 %collective-permute-start.10 = (f32[5,1,128]{2,1,0:T(1,128)S(1)}, f32[5,1,128]{2,1,0:T(1,128)S(1)}, u32[]{:S(2)}, u32[]{:S(2)}) collective-permute-start(f32[5,1,128]{2,1,0:T(1,128)S(1)} %get-tuple-element.54), channel_id=1, source_target_pairs={{2,0},{4,2},{6,4},{3,1},{5,3},{7,5},{10,8},{12,10},{14,12},{11,9},... | collective-permute-start | bytes 7688 | tf_op jit(solution)/shard_map/ppermute | solution.py:31
  128.5 4.5 %collective-permute-start.9 = (f32[5,32,1]{2,1,0:T(8,128)S(1)}, f32[5,32,1]{2,1,0:T(8,128)S(1)}, u32[]{:S(2)}, u32[]{:S(2)}) collective-permute-start(f32[5,32,1]{2,1,0:T(8,128)S(1)} %get-tuple-element.53), channel_id=1, source_target_pairs={{0,1},{1,0},{2,3},{3,2},{4,5},{5,4},{6,7},{7,6},{8,9},{9,8},{10,11... | collective-permute-start | bytes 1928 | tf_op jit(solution)/shard_map/ppermute | solution.py:28
  130.1 5.2 %collective-permute-start.8 = (f32[5,32,1]{2,1,0:T(8,128)S(1)}, f32[5,32,1]{2,1,0:T(8,128)S(1)}, u32[]{:S(2)}, u32[]{:S(2)}) collective-permute-start(f32[5,32,1]{2,1,0:T(8,128)S(1)} %get-tuple-element.52), channel_id=1, source_target_pairs={{1,0},{0,1},{3,2},{2,3},{5,4},{4,5},{7,6},{6,7},{9,8},{8,9},{11,10... | collective-permute-start | bytes 1928 | tf_op jit(solution)/shard_map/ppermute | solution.py:31
  161.7 44.4 %copy-start.11 = (f32[2,32,128]{2,1,0:T(8,128)S(1)}, f32[2,32,128]{2,1,0:T(8,128)}, u32[]{:S(2)}) copy-start(f32[2,32,128]{2,1,0:T(8,128)} %param.12) | copy-start | bytes 98308
  161.7 9.0 %all-to-all-start.2 = ((f32[8,8,128]{2,1,0:T(8,128)}), f32[8,8,128]{2,1,0:T(8,128)S(1)}, u32[]{:S(2)}, u32[]{:S(2)}) async-start(f32[8,8,128]{2,1,0:T(8,128)} %get-tuple-element.40), calls=%async_computation.2 | async-start | bytes 65536 | tf_op jit(solution)/shard_map/all_to_all | solution.py:211
  170.7 36.0 %all-to-all-start.1 = ((f32[32,8,8,128]{3,2,1,0:T(8,128)}), f32[32,8,8,128]{3,2,1,0:T(8,128)S(1)}, u32[]{:S(2)}, u32[]{:S(2)}) async-start(f32[32,8,8,128]{3,2,1,0:T(8,128)} %copy.153), calls=%async_computation.1 | async-start | bytes 2097152 | tf_op jit(solution)/shard_map/all_to_all | solution.py:208
  174.3 9.7 %collective-permute-start.15 = (f32[5,1,128]{2,1,0:T(1,128)S(1)}, f32[5,1,128]{2,1,0:T(1,128)S(1)}, u32[]{:S(2)}, u32[]{:S(2)}) collective-permute-start(f32[5,1,128]{2,1,0:T(1,128)S(1)} %get-tuple-element.49), channel_id=1, source_target_pairs={{0,2},{2,4},{4,6},{1,3},{3,5},{5,7},{8,10},{10,12},{12,14},{9,11},... | collective-permute-start | bytes 7688 | tf_op jit(solution)/shard_map/ppermute | solution.py:28
  175.6 8.4 %collective-permute-start.14 = (f32[5,1,128]{2,1,0:T(1,128)S(1)}, f32[5,1,128]{2,1,0:T(1,128)S(1)}, u32[]{:S(2)}, u32[]{:S(2)}) collective-permute-start(f32[5,1,128]{2,1,0:T(1,128)S(1)} %get-tuple-element.48), channel_id=1, source_target_pairs={{2,0},{4,2},{6,4},{3,1},{5,3},{7,5},{10,8},{12,10},{14,12},{11,9},... | collective-permute-start | bytes 7688 | tf_op jit(solution)/shard_map/ppermute | solution.py:31
  177.0 5.2 %collective-permute-start.13 = (f32[5,32,1]{2,1,0:T(8,128)S(1)}, f32[5,32,1]{2,1,0:T(8,128)S(1)}, u32[]{:S(2)}, u32[]{:S(2)}) collective-permute-start(f32[5,32,1]{2,1,0:T(8,128)S(1)} %get-tuple-element.47), channel_id=1, source_target_pairs={{0,1},{1,0},{2,3},{3,2},{4,5},{5,4},{6,7},{7,6},{8,9},{9,8},{10,11... | collective-permute-start | bytes 1928 | tf_op jit(solution)/shard_map/ppermute | solution.py:28
  178.6 5.4 %collective-permute-start.12 = (f32[5,32,1]{2,1,0:T(8,128)S(1)}, f32[5,32,1]{2,1,0:T(8,128)S(1)}, u32[]{:S(2)}, u32[]{:S(2)}) collective-permute-start(f32[5,32,1]{2,1,0:T(8,128)S(1)} %get-tuple-element.46), channel_id=1, source_target_pairs={{1,0},{0,1},{3,2},{2,3},{5,4},{4,5},{7,6},{6,7},{9,8},{8,9},{11,10... | collective-permute-start | bytes 1928 | tf_op jit(solution)/shard_map/ppermute | solution.py:31
where the time goes:
time: 209 us; the launch traced here: 208 us
  blocking collectives  60 us (29%)
  other arithmetic  45.3 us (22%)
  local copies, waits for them, and re-layouts  38.1 us (18%)
  starting transfers between devices  35.1 us (17%)
  waiting for transfers between devices  26 us (12%)
  matrix products  2.11 us (1%)
    psum x2, blocking collectives, ocean_step(): divergence = lax.psum(partial_div, 'trc')  44.3 us
    mul x4, other arithmetic, face_flux(): return courant * jnp.where(courant >= 0, upwind_pos, upwind_neg)  18.3 us
    ppermute x8, waiting for transfers between devices, padded(): lax.ppermute(lax.slice_in_dim(block, block.shape[dim] - width, None, axis...  16.8 us
    all_gather x1, blocking collectives, body(): lax.all_gather(jnp.stack([east_start, north_start]), 'trc', axis=1, tiled...  15.7 us
    ppermute x8, starting transfers between devices, padded(): lax.ppermute(lax.slice_in_dim(block, block.shape[dim] - width, None, axis...  13.9 us
    ppermute x8, starting transfers between devices, padded(): lax.ppermute(lax.slice_in_dim(block, 0, width, axis=dim), axis, backward)  9.21 us
    ppermute x8, waiting for transfers between devices, padded(): lax.ppermute(lax.slice_in_dim(block, 0, width, axis=dim), axis, backward)  6.48 us
    concatenate x3, other arithmetic, padded(): block = jnp.concatenate([low, block, high], axis=dim)  6.44 us
  transfers between devices with their start and end apart: 19, of which 8 were waited for; matrix products, arithmetic and copies ran while one was open for 19% of the time, Pallas kernels for 0%

commit v1 on v0

--- a/solution.py
+++ b/solution.py
@@ -187,7 +187,11 @@
         zonal_flow_value, meridional_flow_value, free_top_height = ocean_step(
             zonal_flow_value, meridional_flow_value, free_top_height, wet_own, coriolis
         )
-    velocity = lax.all_gather(jnp.stack([east_start, north_start]), "trc", axis=1, tiled=True)
+    payload = jnp.stack([east_start, north_start])
+    answer = lax.axis_size("trc")
+    oldest = jnp.stack([payload] * answer)
+    out_arr = lax.all_to_all(oldest, "trc", 0, 0)
+    velocity = jnp.concatenate(out_arr, axis=1)
     flow = jnp.concatenate([velocity, wet_all[None]], 0)
     flow_ext = widen_flow(flow, 4)
     first = transport(

time: 209 us -> 213 us (1.019)
  blocking collectives: 60 us -> 44.4 us
  waiting for transfers between devices: 26 us -> 33.5 us
  starting transfers between devices: 35.1 us -> 42.1 us
  other arithmetic: 45.3 us -> 47.7 us
  local copies, waits for them, and re-layouts: 38.1 us -> 40.3 us
    all_gather x1 -> x0, blocking collectives: 15.7 us -> none  [body(): lax.all_gather(jnp.stack([east_start, north_start]), 'trc', axis=1, tiled...]
    all_to_all x0 -> x1, starting transfers between devices: none -> 6.35 us  [body(): out_arr = lax.all_to_all(oldest, 'trc', 0, 0)]
    ppermute x8, waiting for transfers between devices: 6.48 us -> 11.4 us  [padded(): lax.ppermute(lax.slice_in_dim(block, 0, width, axis=dim), axis, backward)]
    mul x4, other arithmetic: 18.3 us -> 22.8 us  [face_flux(): return courant * jnp.where(courant >= 0, upwind_pos, upwind_neg)]
    ppermute x8, waiting for transfers between devices: 16.8 us -> 19.4 us  [padded(): lax.ppermute(lax.slice_in_dim(block, block.shape[dim] - width, None, axis...]
  transfers between devices with their start and end apart: 19 -> 20, of which waited for: 8 -> 9; matrix products, arithmetic and copies ran while one was open for 19% -> 11% of each run, Pallas kernels for 0% -> 0%
where the time goes in v1:
time: 213 us; the launch traced here: 211 us
  other arithmetic  47.7 us (22%)
  blocking collectives  44.4 us (21%)
  starting transfers between devices  42.1 us (20%)
  local copies, waits for them, and re-layouts  40.3 us (19%)
  waiting for transfers between devices  33.5 us (16%)
    psum x2, blocking collectives, ocean_step(): divergence = lax.psum(partial_div, 'trc')  44.4 us
    mul x4, other arithmetic, face_flux(): return courant * jnp.where(courant >= 0, upwind_pos, upwind_neg)  22.8 us
    ppermute x8, waiting for transfers between devices, padded(): lax.ppermute(lax.slice_in_dim(block, block.shape[dim] - width, None, axis...  19.4 us
    ppermute x8, starting transfers between devices, padded(): lax.ppermute(lax.slice_in_dim(block, block.shape[dim] - width, None, axis...  14.4 us
    ppermute x8, waiting for transfers between devices, padded(): lax.ppermute(lax.slice_in_dim(block, 0, width, axis=dim), axis, backward)  11.4 us
    ppermute x8, starting transfers between devices, padded(): lax.ppermute(lax.slice_in_dim(block, 0, width, axis=dim), axis, backward)  9.35 us
    mul x4, local copies, waits for them, and re-layouts, face_flux(): 0.5 * (1.0 - courant) * limited_slope(after - center, center - before)  7.63 us
    sub x2, other arithmetic, transport(): field[..., rows, cols] - (flux_x[..., 1:] - flux_x[..., :-1])  6.68 us
  transfers between devices with their start and end apart: 20, of which 9 were waited for; matrix products, arithmetic and copies ran while one was open for 11% of the time, Pallas kernels for 0%

profile of v1, /device:TPU:0, one launch (start us, length us, event | category | flops | bytes accessed | tf_op | source)
XLA Modules:
  0.0 211.4 jit_solution(776296008972280988)
XLA Ops:
  3.0 6.3 %all-to-all-start = ((f32[4,2,2,32,128]{4,3,2,1,0:T(8,128)}), f32[4,2,2,32,128]{4,3,2,1,0:T(8,128)S(1)}, u32[]{:S(2)}, u32[]{:S(2)}) async-start(f32[4,2,2,32,128]{4,3,2,1,0:T(8,128)} %stack.19), calls=%async_computation | async-start | bytes 524288 | tf_op jit(solution)/shard_map/all_to_all | solution.py:193
  10.4 1.3 collective-permute-start.1
  11.8 3.0 %collective-permute-start = (f32[8,8,4,128]{3,1,2,0:T(8,128)S(1)}, f32[8,8,4,128]{3,1,2,0:T(8,128)S(1)}, u32[]{:S(2)}, u32[]{:S(2)}) collective-permute-start(f32[8,8,4,128]{3,1,2,0:T(8,128)S(1)} %copy.139), channel_id=1, source_target_pairs={{0,2},{2,4},{4,6},{1,3},{3,5},{5,7},{8,10},{10,12},{12,14},{9,11},... | collective-permute-start | bytes 393224 | tf_op jit(solution)/shard_map/ppermute | solution.py:28
  14.8 3.7 %copy.111 = f32[8,8,32,128]{2,1,3,0:T(8,128)} copy(f32[8,8,32,128]{3,2,1,0:T(8,128)} %param.9) | data formatting | bytes 2097152 | tf_op args[0]
  18.5 2.7 %copy.112 = f32[8,8,4,128]{2,1,3,0:T(8,128)} copy(f32[8,8,4,128]{3,1,2,0:T(8,128)S(1)} %collective-permute-done.1) | data formatting | bytes 262144 | tf_op jit(solution)/shard_map/ppermute | solution.py:31
  21.2 2.8 %copy.110 = f32[8,8,4,128]{2,1,3,0:T(8,128)} copy(f32[8,8,4,128]{3,1,2,0:T(8,128)S(1)} %collective-permute-done) | data formatting | bytes 262144 | tf_op jit(solution)/shard_map/ppermute | solution.py:28
  24.2 1.3 collective-permute-start.5
  25.5 3.6 %collective-permute-start.4 = (f32[3,8,4,128]{3,1,2,0:T(8,128)S(1)}, f32[3,8,4,128]{3,1,2,0:T(8,128)S(1)}, u32[]{:S(2)}, u32[]{:S(2)}) collective-permute-start(f32[3,8,4,128]{3,1,2,0:T(8,128)S(1)} %get-tuple-element.25), channel_id=1, source_target_pairs={{0,2},{2,4},{4,6},{1,3},{3,5},{5,7},{8,10},{10,12},{12,14},{9,11},... | collective-permute-start | bytes 147464 | tf_op jit(solution)/shard_map/ppermute | solution.py:28
  29.2 1.6 pad_maximum_fusion.5
  30.7 1.6 collective-permute-start.3
  33.1 1.6 collective-permute-start.7
  36.4 2.8 %collective-permute-done.2 = f32[8,8,40,4]{2,1,3,0:T(8,128)S(1)} collective-permute-done((f32[8,8,40,4]{2,1,3,0:T(8,128)S(1)}, f32[8,8,40,4]{2,1,3,0:T(8,128)S(1)}, u32[]{:S(2)}, u32[]{:S(2)}) %collective-permute-start.2) | collective-permute-done | bytes 40992 | tf_op jit(solution)/shard_map/ppermute | solution.py:28
  39.2 3.9 %pad_maximum_fusion = f32[8,8,40,136]{2,1,3,0:T(8,128)} fusion(f32[8,8,40,4]{2,1,3,0:T(8,128)S(1)} %collective-permute-done.3, f32[8,8,4,128]{2,1,3,0:T(8,128)S(1)} %copy-done.2, f32[8,8,32,128]{2,1,3,0:T(8,128)S(1)} %copy-done.1, f32[8,8,4,128]{2,1,3,0:T(8,128)S(1)} %copy-done.3, f32[8,8,40,4]{2,1,3,0:T(8,128)S(1)} %collective-permute-done.2), kind=kLoop, calls=%fused_computation.8 | loop fusion | flops 1392640 | bytes 2785280 | tf_op jit(solution)/shard_map/concatenate | solution.py:32
  43.1 6.6 %collective-permute-done.7 = f32[3,8,40,4]{3,1,2,0:T(8,128)S(1)} collective-permute-done((f32[3,8,40,4]{3,1,2,0:T(8,128)S(1)}, f32[3,8,40,4]{3,1,2,0:T(8,128)S(1)}, u32[]{:S(2)}, u32[]{:S(2)}) %collective-permute-start.7) | collective-permute-done | bytes 15392 | tf_op jit(solution)/shard_map/ppermute | solution.py:31
  49.7 10.5 %collective-permute-done.6 = f32[3,8,40,4]{3,1,2,0:T(8,128)S(1)} collective-permute-done((f32[3,8,40,4]{3,1,2,0:T(8,128)S(1)}, f32[3,8,40,4]{3,1,2,0:T(8,128)S(1)}, u32[]{:S(2)}, u32[]{:S(2)}) %collective-permute-start.6) | collective-permute-done | bytes 15392 | tf_op jit(solution)/shard_map/ppermute | solution.py:28
  70.7 1.4 copy.122
  72.1 2.1 %copy.121 = f32[8,37,132]{1,0,2:T(8,128)} copy(f32[8,37,132]{2,0,1:T(8,128)} %get-tuple-element.27) | data formatting | bytes 312576 | tf_op jit(solution)/shard_map/mul | solution.py:45
  75.3 1.4 copy.118
  76.7 1.4 copy.117
  78.1 1.3 copy.116
  79.4 1.9 copy.130
  81.3 2.0 copy.129
  83.3 1.7 copy.128
  86.1 2.2 %copy.125 = f32[8,32,129]{1,0,2:T(8,128)} copy(f32[8,32,129]{2,0,1:T(8,128)} %get-tuple-element.31) | data formatting | bytes 264192 | tf_op jit(solution)/shard_map/mul | solution.py:45
  89.4 9.0 %fusion.12 = f32[8,8,37,132]{2,1,3,0:T(8,128)S(1)} fusion(f32[8,8,40,136]{2,1,3,0:T(8,128)} %pad_maximum_fusion, f32[8,37,132]{1,0,2:T(8,128)S(1)} %copy.122, f32[8,37,132]{1,0,2:T(8,128)} %copy.121, f32[8,37,132]{1,0,2:T(8,128)S(1)} %copy.119, pred[8,37,132]{1,0,2:T(8,128)(4,1)} %copy.120), kind=kLoop, calls=%fused_computation.26 | loop fusion | flops 8126976 | bytes 6759456 | tf_op jit(solution)/shard_map/mul | solution.py:47
  98.4 4.9 %fusion.4 = f32[8,8,36,133]{2,1,3,0:T(8,128)S(1)} fusion(f32[8,8,40,136]{2,1,3,0:T(8,128)S(1)} %bitcast.71, f32[8,36,133]{1,0,2:T(8,128)S(1)} %copy.118, f32[8,36,133]{1,0,2:T(8,128)S(1)} %copy.117, f32[8,36,133]{1,0,2:T(8,128)S(1)} %copy.115, pred[8,36,133]{1,0,2:T(8,128)(4,1)S(1)} %copy.116), kind=kLoop, calls=%fused_computation.13 | loop fusion | flops 7967232 | bytes 6626592 | tf_op jit(solution)/shard_map/mul | solution.py:47
  103.3 2.9 %fusion.16 = f32[8,8,36,132]{2,1,3,0:T(8,128)S(1)} fusion(f32[8,8,37,132]{2,1,3,0:T(8,128)S(1)} %fusion.12, f32[8,8,36,133]{2,1,3,0:T(8,128)S(1)} %fusion.4, f32[8,8,40,136]{2,1,3,0:T(8,128)S(1)} %bitcast.71), kind=kLoop, calls=%fused_computation.31 | loop fusion | flops 1216512 | bytes 7299072 | tf_op jit(solution)/shard_map/sub | solution.py:75
  106.3 4.2 %fusion.30 = f32[8,8,33,128]{2,1,3,0:T(8,128)S(1)} fusion(f32[8,8,36,132]{2,1,3,0:T(8,128)S(1)} %fusion.16, f32[8,33,128]{1,0,2:T(8,128)S(1)} %copy-done.8, f32[8,33,128]{1,0,2:T(8,128)S(1)} %copy-done.9, f32[8,33,128]{1,0,2:T(8,128)S(1)} %copy-done.7, pred[8,33,128]{1,0,2:T(8,128)(4,1)S(1)} %copy-done.13), kind=kLoop, calls=%fused_computation.56 | loop fusion | flops 7028736 | bytes 5846016 | tf_op jit(solution)/shard_map/mul | solution.py:47
  110.6 4.7 %fusion.22 = f32[8,8,32,129]{2,1,3,0:T(8,128)S(1)} fusion(f32[8,8,36,132]{2,1,3,0:T(8,128)S(1)} %fusion.16, f32[8,32,129]{1,0,2:T(8,128)S(1)} %copy-done.5, f32[8,32,129]{1,0,2:T(8,128)S(1)} %copy-done.6, f32[8,32,129]{1,0,2:T(8,128)S(1)} %copy-done.4, pred[8,32,129]{1,0,2:T(8,128)(4,1)S(1)} %copy-done.12), kind=kLoop, calls=%fused_computation.43 | loop fusion | flops 6868992 | bytes 5713152 | tf_op jit(solution)/shard_map/mul | solution.py:47
  115.3 3.8 %fusion.34 = f32[8,8,32,128]{2,1,3,0:T(8,128)} fusion(f32[8,8,33,128]{2,1,3,0:T(8,128)S(1)} %fusion.30, f32[8,8,32,129]{2,1,3,0:T(8,128)S(1)} %fusion.22, f32[8,8,36,132]{2,1,3,0:T(8,128)S(1)} %fusion.16), kind=kLoop, calls=%fused_computation.61 | loop fusion | flops 1048576 | bytes 6291456 | tf_op jit(solution)/shard_map/sub | solution.py:75
  119.1 3.9 %copy.131 = f32[8,8,32,128]{3,1,0,2:T(8,128)} copy(f32[8,8,32,128]{2,1,3,0:T(8,128)} %fusion.34) | data formatting | bytes 2097152 | tf_op jit(solution)/shard_map/sub | solution.py:75
  123.0 5.1 %all-to-all-start.1 = ((f32[8,8,32,128]{3,1,0,2:T(8,128)}), f32[8,8,32,128]{3,1,0,2:T(8,128)S(1)}, u32[]{:S(2)}, u32[]{:S(2)}) async-start(f32[8,8,32,128]{3,1,0,2:T(8,128)} %copy.131), calls=%async_computation.1 | async-start | bytes 2097152 | tf_op jit(solution)/shard_map/all_to_all | solution.py:203
  128.1 2.2 %collective-permute-start.11 = (f32[5,1,128]{2,1,0:T(1,128)S(1)}, f32[5,1,128]{2,1,0:T(1,128)S(1)}, u32[]{:S(2)}, u32[]{:S(2)}) collective-permute-start(f32[5,1,128]{2,1,0:T(1,128)S(1)} %get-tuple-element.50), channel_id=1, source_target_pairs={{0,2},{2,4},{4,6},{1,3},{3,5},{5,7},{8,10},{10,12},{12,14},{9,11},... | collective-permute-start | bytes 7688 | tf_op jit(solution)/shard_map/ppermute | solution.py:28
  130.4 1.3 collective-permute-start.10
  131.8 1.6 collective-permute-start.9
  134.0 3.0 %collective-permute-done.9 = f32[5,32,1]{2,1,0:T(8,128)S(1)} collective-permute-done((f32[5,32,1]{2,1,0:T(8,128)S(1)}, f32[5,32,1]{2,1,0:T(8,128)S(1)}, u32[]{:S(2)}, u32[]{:S(2)}) %collective-permute-start.9) | collective-permute-done | bytes 672 | tf_op jit(solution)/shard_map/ppermute | solution.py:28
  137.0 1.8 collective-permute-done.8
  138.9 24.3 %psum.14 = f32[32,128]{1,0:T(8,128)S(1)} all-reduce(f32[32,128]{1,0:T(8,128)S(1)} %multiply_reduce_fusion.1), channel_id=1, replica_groups=mesh['trc'=4,'lat'=4,'lon'=2] {'trc'}, use_global_device_ids=true, to_apply=%region_2.0 | all-reduce | flops 4096 | bytes 32768 | tf_op jit(solution)/shard_map/psum | solution.py:135
  165.0 3.4 %all-to-all-start.3 = ((f32[8,8,128]{2,1,0:T(8,128)}), f32[8,8,128]{2,1,0:T(8,128)S(1)}, u32[]{:S(2)}, u32[]{:S(2)}) async-start(f32[8,8,128]{2,1,0:T(8,128)} %get-tuple-element.35), calls=%async_computation.3 | async-start | bytes 65536 | tf_op jit(solution)/shard_map/all_to_all | solution.py:215
  168.4 1.3 fusion.38
  169.7 1.6 copy.133
  171.3 2.7 %all-to-all-done.3 = f32[8,8,128]{2,1,0:T(8,128)S(1)} async-done(((f32[8,8,128]{2,1,0:T(8,128)}), f32[8,8,128]{2,1,0:T(8,128)S(1)}, u32[]{:S(2)}, u32[]{:S(2)}) %all-to-all-start.3) | async-done | bytes 32800 | tf_op jit(solution)/shard_map/all_to_all | solution.py:215
  174.0 3.5 %all-to-all-start.2 = ((f32[32,8,8,128]{3,2,1,0:T(8,128)}), f32[32,8,8,128]{3,2,1,0:T(8,128)S(1)}, u32[]{:S(2)}, u32[]{:S(2)}) async-start(f32[32,8,8,128]{3,2,1,0:T(8,128)} %copy.133), calls=%async_computation.2 | async-start | bytes 2097152 | tf_op jit(solution)/shard_map/all_to_all | solution.py:212
  178.8 1.3 collective-permute-start.14
  180.2 1.6 collective-permute-start.13
  182.3 3.1 %collective-permute-done.13 = f32[5,32,1]{2,1,0:T(8,128)S(1)} collective-permute-done((f32[5,32,1]{2,1,0:T(8,128)S(1)}, f32[5,32,1]{2,1,0:T(8,128)S(1)}, u32[]{:S(2)}, u32[]{:S(2)}) %collective-permute-start.13) | collective-permute-done | bytes 672 | tf_op jit(solution)/shard_map/ppermute | solution.py:28
  185.5 1.8 collective-permute-done.12
  187.3 20.2 %psum.15 = f32[32,128]{1,0:T(8,128)S(1)} all-reduce(f32[32,128]{1,0:T(8,128)S(1)} %multiply_reduce_fusion), channel_id=1, replica_groups=mesh['trc'=4,'lat'=4,'lon'=2] {'trc'}, use_global_device_ids=true, to_apply=%region_4.5 | all-reduce | flops 4096 | bytes 32768 | tf_op jit(solution)/shard_map/psum | solution.py:135
  (114 shorter events, 28.5 us)
Async XLA Ops:
  0.6 167.7 %copy-start = (f32[32,32]{1,0:T(8,128)S(1)}, f32[32,32]{1,0:T(8,128)}, u32[]{:S(2)}) copy-start(f32[32,32]{1,0:T(8,128)} %param.15) | copy-start | bytes 12292
  0.6 17.8 %copy-start.15 = (s32[32,128]{1,0:T(8,128)S(1)}, s32[32,128]{1,0:T(8,128)}, u32[]{:S(2)}) copy-start(s32[32,128]{1,0:T(8,128)} %param.14) | copy-start | bytes 49156
  3.0 21.0 %all-to-all-start = ((f32[4,2,2,32,128]{4,3,2,1,0:T(8,128)}), f32[4,2,2,32,128]{4,3,2,1,0:T(8,128)S(1)}, u32[]{:S(2)}, u32[]{:S(2)}) async-start(f32[4,2,2,32,128]{4,3,2,1,0:T(8,128)} %stack.19), calls=%async_computation | async-start | bytes 524288 | tf_op jit(solution)/shard_map/all_to_all | solution.py:193
  10.4 8.1 %collective-permute-start.1 = (f32[8,8,4,128]{3,1,2,0:T(8,128)S(1)}, f32[8,8,4,128]{3,1,2,0:T(8,128)S(1)}, u32[]{:S(2)}, u32[]{:S(2)}) collective-permute-start(f32[8,8,4,128]{3,1,2,0:T(8,128)S(1)} %copy.140), channel_id=1, source_target_pairs={{2,0},{4,2},{6,4},{3,1},{5,3},{7,5},{10,8},{12,10},{14,12},{11,9},... | collective-permute-start | bytes 393224 | tf_op jit(solution)/shard_map/ppermute | solution.py:31
  11.8 9.5 %collective-permute-start = (f32[8,8,4,128]{3,1,2,0:T(8,128)S(1)}, f32[8,8,4,128]{3,1,2,0:T(8,128)S(1)}, u32[]{:S(2)}, u32[]{:S(2)}) collective-permute-start(f32[8,8,4,128]{3,1,2,0:T(8,128)S(1)} %copy.139), channel_id=1, source_target_pairs={{0,2},{2,4},{4,6},{1,3},{3,5},{5,7},{8,10},{10,12},{12,14},{9,11},... | collective-permute-start | bytes 393224 | tf_op jit(solution)/shard_map/ppermute | solution.py:28
  24.2 8.6 %collective-permute-start.5 = (f32[3,8,4,128]{3,1,2,0:T(8,128)S(1)}, f32[3,8,4,128]{3,1,2,0:T(8,128)S(1)}, u32[]{:S(2)}, u32[]{:S(2)}) collective-permute-start(f32[3,8,4,128]{3,1,2,0:T(8,128)S(1)} %get-tuple-element.26), channel_id=1, source_target_pairs={{2,0},{4,2},{6,4},{3,1},{5,3},{7,5},{10,8},{12,10},{14,12},{11,9},... | collective-permute-start | bytes 147464 | tf_op jit(solution)/shard_map/ppermute | solution.py:31
  25.5 7.3 %collective-permute-start.4 = (f32[3,8,4,128]{3,1,2,0:T(8,128)S(1)}, f32[3,8,4,128]{3,1,2,0:T(8,128)S(1)}, u32[]{:S(2)}, u32[]{:S(2)}) collective-permute-start(f32[3,8,4,128]{3,1,2,0:T(8,128)S(1)} %get-tuple-element.25), channel_id=1, source_target_pairs={{0,2},{2,4},{4,6},{1,3},{3,5},{5,7},{8,10},{10,12},{12,14},{9,11},... | collective-permute-start | bytes 147464 | tf_op jit(solution)/shard_map/ppermute | solution.py:28
  29.1 10.1 %copy-start.1 = (f32[8,8,32,128]{2,1,3,0:T(8,128)S(1)}, f32[8,8,32,128]{2,1,3,0:T(8,128)}, u32[]{:S(2)}) copy-start(f32[8,8,32,128]{2,1,3,0:T(8,128)} %copy.111) | copy-start | bytes 3145732
  29.2 10.1 %copy-start.2 = (f32[8,8,4,128]{2,1,3,0:T(8,128)S(1)}, f32[8,8,4,128]{2,1,3,0:T(8,128)}, u32[]{:S(2)}) copy-start(f32[8,8,4,128]{2,1,3,0:T(8,128)} %copy.112) | copy-start | bytes 393220
  29.2 10.1 %copy-start.3 = (f32[8,8,4,128]{2,1,3,0:T(8,128)S(1)}, f32[8,8,4,128]{2,1,3,0:T(8,128)}, u32[]{:S(2)}) copy-start(f32[8,8,4,128]{2,1,3,0:T(8,128)} %copy.110) | copy-start | bytes 393220
  30.7 5.7 %collective-permute-start.3 = (f32[8,8,40,4]{2,1,3,0:T(8,128)S(1)}, f32[8,8,40,4]{2,1,3,0:T(8,128)S(1)}, u32[]{:S(2)}, u32[]{:S(2)}) collective-permute-start(f32[8,8,40,4]{2,1,3,0:T(8,128)S(1)} %get-tuple-element.14), channel_id=1, source_target_pairs={{1,0},{0,1},{3,2},{2,3},{5,4},{4,5},{7,6},{6,7},{9,8},{8,9},{11,10... | collective-permute-start | bytes 122888 | tf_op jit(solution)/shard_map/ppermute | solution.py:31
  32.3 6.9 %collective-permute-start.2 = (f32[8,8,40,4]{2,1,3,0:T(8,128)S(1)}, f32[8,8,40,4]{2,1,3,0:T(8,128)S(1)}, u32[]{:S(2)}, u32[]{:S(2)}) collective-permute-start(f32[8,8,40,4]{2,1,3,0:T(8,128)S(1)} %get-tuple-element.13), channel_id=1, source_target_pairs={{0,1},{1,0},{2,3},{3,2},{4,5},{5,4},{6,7},{7,6},{8,9},{9,8},{10,11... | collective-permute-start | bytes 122888 | tf_op jit(solution)/shard_map/ppermute | solution.py:28
  33.1 16.7 %collective-permute-start.7 = (f32[3,8,40,4]{3,1,2,0:T(8,128)S(1)}, f32[3,8,40,4]{3,1,2,0:T(8,128)S(1)}, u32[]{:S(2)}, u32[]{:S(2)}) collective-permute-start(f32[3,8,40,4]{3,1,2,0:T(8,128)S(1)} %get-tuple-element.24), channel_id=1, source_target_pairs={{1,0},{0,1},{3,2},{2,3},{5,4},{4,5},{7,6},{6,7},{9,8},{8,9},{11,10... | collective-permute-start | bytes 46088 | tf_op jit(solution)/shard_map/ppermute | solution.py:31
  34.7 25.6 %collective-permute-start.6 = (f32[3,8,40,4]{3,1,2,0:T(8,128)S(1)}, f32[3,8,40,4]{3,1,2,0:T(8,128)S(1)}, u32[]{:S(2)}, u32[]{:S(2)}) collective-permute-start(f32[3,8,40,4]{3,1,2,0:T(8,128)S(1)} %get-tuple-element.23), channel_id=1, source_target_pairs={{0,1},{1,0},{2,3},{3,2},{4,5},{5,4},{6,7},{7,6},{8,9},{9,8},{10,11... | collective-permute-start | bytes 46088 | tf_op jit(solution)/shard_map/ppermute | solution.py:28
  68.7 19.6 %copy-start.14 = (pred[8,32,129]{2,0,1:T(8,128)(4,1)S(1)}, pred[8,32,129]{2,0,1:T(8,128)(4,1)}, u32[]{:S(2)}) copy-start(pred[8,32,129]{2,0,1:T(8,128)(4,1)} %get-tuple-element.5) | copy-start | bytes 99076
  70.7 14.2 %copy-start.10 = (f32[8,32,129]{2,0,1:T(8,128)S(1)}, f32[8,32,129]{2,0,1:T(8,128)}, u32[]{:S(2)}) copy-start(f32[8,32,129]{2,0,1:T(8,128)} %get-tuple-element.32) | copy-start | bytes 396292
  86.1 12.2 %slice-start = ((s8[4456448]{0:T(1024)(128)(4,1)}), s8[262144]{0:T(1024)(128)(4,1)S(1)}, s32[]{:S(2)}) async-start(s8[4456448]{0:T(1024)(128)(4,1)} %bitcast.70), calls=%async_computation.4 | async-start | bytes 524288
  89.4 9.0 %slice-start.1 = ((s8[4456448]{0:T(1024)(128)(4,1)}), s8[4194304]{0:T(1024)(128)(4,1)S(1)}, s32[]{:S(2)}) async-start(s8[4456448]{0:T(1024)(128)(4,1)} %bitcast.70), calls=%async_computation.5 | async-start | bytes 8388608
  103.3 2.9 %copy-start.7 = (f32[8,33,128]{1,0,2:T(8,128)S(1)}, f32[8,33,128]{1,0,2:T(8,128)}, u32[]{:S(2)}) copy-start(f32[8,33,128]{1,0,2:T(8,128)} %copy.127) | copy-start | bytes 405508
  103.3 2.9 %copy-start.8 = (f32[8,33,128]{1,0,2:T(8,128)S(1)}, f32[8,33,128]{1,0,2:T(8,128)}, u32[]{:S(2)}) copy-start(f32[8,33,128]{1,0,2:T(8,128)} %copy.130) | copy-start | bytes 405508
  103.3 2.9 %copy-start.9 = (f32[8,33,128]{1,0,2:T(8,128)S(1)}, f32[8,33,128]{1,0,2:T(8,128)}, u32[]{:S(2)}) copy-start(f32[8,33,128]{1,0,2:T(8,128)} %copy.129) | copy-start | bytes 405508
  103.3 2.9 %copy-start.13 = (pred[8,33,128]{1,0,2:T(8,128)(4,1)S(1)}, pred[8,33,128]{1,0,2:T(8,128)(4,1)}, u32[]{:S(2)}) copy-start(pred[8,33,128]{1,0,2:T(8,128)(4,1)} %copy.128) | copy-start | bytes 101380
  106.2 4.3 %copy-start.4 = (f32[8,32,129]{1,0,2:T(8,128)S(1)}, f32[8,32,129]{1,0,2:T(8,128)}, u32[]{:S(2)}) copy-start(f32[8,32,129]{1,0,2:T(8,128)} %copy.123) | copy-start | bytes 396292
  106.3 4.3 %copy-start.5 = (f32[8,32,129]{1,0,2:T(8,128)S(1)}, f32[8,32,129]{1,0,2:T(8,128)}, u32[]{:S(2)}) copy-start(f32[8,32,129]{1,0,2:T(8,128)} %copy.126) | copy-start | bytes 396292
  106.3 4.3 %copy-start.6 = (f32[8,32,129]{1,0,2:T(8,128)S(1)}, f32[8,32,129]{1,0,2:T(8,128)}, u32[]{:S(2)}) copy-start(f32[8,32,129]{1,0,2:T(8,128)} %copy.125) | copy-start | bytes 396292
  106.3 4.3 %copy-start.12 = (pred[8,32,129]{1,0,2:T(8,128)(4,1)S(1)}, pred[8,32,129]{1,0,2:T(8,128)(4,1)}, u32[]{:S(2)}) copy-start(pred[8,32,129]{1,0,2:T(8,128)(4,1)} %copy.124) | copy-start | bytes 99076
  119.1 9.0 %copy-start.11 = (f32[32,128]{1,0:T(8,128)S(1)}, f32[32,128]{1,0:T(8,128)}, u32[]{:S(2)}) copy-start(f32[32,128]{1,0:T(8,128)} %param.13) | copy-start | bytes 49156
  119.1 44.4 %copy-start.17 = (f32[32]{0:T(128)S(1)}, f32[32]{0:T(128)}, u32[]{:S(2)}) copy-start(f32[32]{0:T(128)} %param.17) | copy-start | bytes 388
  119.1 49.3 %copy-start.18 = (f32[32]{0:T(128)S(1)}, f32[32]{0:T(128)}, u32[]{:S(2)}) copy-start(f32[32]{0:T(128)} %param.16) | copy-start | bytes 388
  123.0 40.4 %all-to-all-start.1 = ((f32[8,8,32,128]{3,1,0,2:T(8,128)}), f32[8,8,32,128]{3,1,0,2:T(8,128)S(1)}, u32[]{:S(2)}, u32[]{:S(2)}) async-start(f32[8,8,32,128]{3,1,0,2:T(8,128)} %copy.131), calls=%async_computation.1 | async-start | bytes 2097152 | tf_op jit(solution)/shard_map/all_to_all | solution.py:203
  128.1 10.6 %collective-permute-start.11 = (f32[5,1,128]{2,1,0:T(1,128)S(1)}, f32[5,1,128]{2,1,0:T(1,128)S(1)}, u32[]{:S(2)}, u32[]{:S(2)}) collective-permute-start(f32[5,1,128]{2,1,0:T(1,128)S(1)} %get-tuple-element.50), channel_id=1, source_target_pairs={{0,2},{2,4},{4,6},{1,3},{3,5},{5,7},{8,10},{10,12},{12,14},{9,11},... | collective-permute-start | bytes 7688 | tf_op jit(solution)/shard_map/ppermute | solution.py:28
  130.4 8.4 %collective-permute-start.10 = (f32[5,1,128]{2,1,0:T(1,128)S(1)}, f32[5,1,128]{2,1,0:T(1,128)S(1)}, u32[]{:S(2)}, u32[]{:S(2)}) collective-permute-start(f32[5,1,128]{2,1,0:T(1,128)S(1)} %get-tuple-element.49), channel_id=1, source_target_pairs={{2,0},{4,2},{6,4},{3,1},{5,3},{7,5},{10,8},{12,10},{14,12},{11,9},... | collective-permute-start | bytes 7688 | tf_op jit(solution)/shard_map/ppermute | solution.py:31
  131.8 5.2 %collective-permute-start.9 = (f32[5,32,1]{2,1,0:T(8,128)S(1)}, f32[5,32,1]{2,1,0:T(8,128)S(1)}, u32[]{:S(2)}, u32[]{:S(2)}) collective-permute-start(f32[5,32,1]{2,1,0:T(8,128)S(1)} %get-tuple-element.48), channel_id=1, source_target_pairs={{0,1},{1,0},{2,3},{3,2},{4,5},{5,4},{6,7},{7,6},{8,9},{9,8},{10,11... | collective-permute-start | bytes 1928 | tf_op jit(solution)/shard_map/ppermute | solution.py:28
  133.3 5.4 %collective-permute-start.8 = (f32[5,32,1]{2,1,0:T(8,128)S(1)}, f32[5,32,1]{2,1,0:T(8,128)S(1)}, u32[]{:S(2)}, u32[]{:S(2)}) collective-permute-start(f32[5,32,1]{2,1,0:T(8,128)S(1)} %get-tuple-element.47), channel_id=1, source_target_pairs={{1,0},{0,1},{3,2},{2,3},{5,4},{4,5},{7,6},{6,7},{9,8},{8,9},{11,10... | collective-permute-start | bytes 1928 | tf_op jit(solution)/shard_map/ppermute | solution.py:31
  165.0 44.7 %copy-start.16 = (f32[2,32,128]{2,1,0:T(8,128)S(1)}, f32[2,32,128]{2,1,0:T(8,128)}, u32[]{:S(2)}) copy-start(f32[2,32,128]{2,1,0:T(8,128)} %param.12) | copy-start | bytes 98308
  165.0 9.0 %all-to-all-start.3 = ((f32[8,8,128]{2,1,0:T(8,128)}), f32[8,8,128]{2,1,0:T(8,128)S(1)}, u32[]{:S(2)}, u32[]{:S(2)}) async-start(f32[8,8,128]{2,1,0:T(8,128)} %get-tuple-element.35), calls=%async_computation.3 | async-start | bytes 65536 | tf_op jit(solution)/shard_map/all_to_all | solution.py:215
  174.0 36.3 %all-to-all-start.2 = ((f32[32,8,8,128]{3,2,1,0:T(8,128)}), f32[32,8,8,128]{3,2,1,0:T(8,128)S(1)}, u32[]{:S(2)}, u32[]{:S(2)}) async-start(f32[32,8,8,128]{3,2,1,0:T(8,128)} %copy.133), calls=%async_computation.2 | async-start | bytes 2097152 | tf_op jit(solution)/shard_map/all_to_all | solution.py:212
  177.5 9.7 %collective-permute-start.15 = (f32[5,1,128]{2,1,0:T(1,128)S(1)}, f32[5,1,128]{2,1,0:T(1,128)S(1)}, u32[]{:S(2)}, u32[]{:S(2)}) collective-permute-start(f32[5,1,128]{2,1,0:T(1,128)S(1)} %get-tuple-element.44), channel_id=1, source_target_pairs={{0,2},{2,4},{4,6},{1,3},{3,5},{5,7},{8,10},{10,12},{12,14},{9,11},... | collective-permute-start | bytes 7688 | tf_op jit(solution)/shard_map/ppermute | solution.py:28
  178.8 8.4 %collective-permute-start.14 = (f32[5,1,128]{2,1,0:T(1,128)S(1)}, f32[5,1,128]{2,1,0:T(1,128)S(1)}, u32[]{:S(2)}, u32[]{:S(2)}) collective-permute-start(f32[5,1,128]{2,1,0:T(1,128)S(1)} %get-tuple-element.43), channel_id=1, source_target_pairs={{2,0},{4,2},{6,4},{3,1},{5,3},{7,5},{10,8},{12,10},{14,12},{11,9},... | collective-permute-start | bytes 7688 | tf_op jit(solution)/shard_map/ppermute | solution.py:31
  180.2 5.2 %collective-permute-start.13 = (f32[5,32,1]{2,1,0:T(8,128)S(1)}, f32[5,32,1]{2,1,0:T(8,128)S(1)}, u32[]{:S(2)}, u32[]{:S(2)}) collective-permute-start(f32[5,32,1]{2,1,0:T(8,128)S(1)} %get-tuple-element.42), channel_id=1, source_target_pairs={{0,1},{1,0},{2,3},{3,2},{4,5},{5,4},{6,7},{7,6},{8,9},{9,8},{10,11... | collective-permute-start | bytes 1928 | tf_op jit(solution)/shard_map/ppermute | solution.py:28
  181.8 5.4 %collective-permute-start.12 = (f32[5,32,1]{2,1,0:T(8,128)S(1)}, f32[5,32,1]{2,1,0:T(8,128)S(1)}, u32[]{:S(2)}, u32[]{:S(2)}) collective-permute-start(f32[5,32,1]{2,1,0:T(8,128)S(1)} %get-tuple-element.41), channel_id=1, source_target_pairs={{1,0},{0,1},{3,2},{2,3},{5,4},{4,5},{7,6},{6,7},{9,8},{8,9},{11,10... | collective-permute-start | bytes 1928 | tf_op jit(solution)/shard_map/ppermute | solution.py:31
